TPU v7x, 512 devices: a whole 4x4x16 slice. The times are simulated.
512 devices in a mesh: row: 64 (over x, z), col: 8 (over y, core).
Axes of the slice: x: 4, y: 4, z: 16, core: 2. Of those that a mesh axis runs over, the one named last changes fastest.
Arguments:
- pending: bfloat16 [65536, 8, 1024], P('row', 'col'), may hold values from -5 to 5
- panel: bfloat16 [65536, 2, 1024], P('row', None, 'col'), may hold values from -0.1875 to 0.1875
- panel_scale: float32 [65536, 2], P('row'), may hold values from 0.1 to 1
- inverse_blocks: bfloat16 [2, 1024, 1024], P(None, 'col'), as said below
Outputs:
- remaining: bfloat16 [65536, 8, 1024], P('row', 'col')
- solved: bfloat16 [2, 1024, 1024], P(None, 'col')
Inputs may be any that keep to these rules, and one draw needn't show every extreme that they name: `inverse_blocks`: each block is lower triangular with a positive diagonal, the inverse of a diagonal block of a Cholesky factor.
All inputs are finite; a program needn't handle non-finite values.
Results may differ from a plain program's by a relative error of at most 0.023.
Values may be sent and summed in bfloat16 or wider, within the bound.
A program may use at most 64 MiB of HBM per device.

v0:
```python
import jax
import jax.numpy as jnp
from jax import lax
from jax.sharding import PartitionSpec as P


def spread(shard, axis, root):
    mine = lax.axis_index(axis) == root
    return lax.psum(jnp.where(mine, shard, jnp.zeros_like(shard)), axis)


def body(pending, panel, panel_scale, inverse_blocks):
    row_index = lax.axis_index("row")
    n_row = lax.axis_size("row")
    block = inverse_blocks.shape[2]
    total = pending.shape[0]
    current = pending[:, 0, :]
    slot_of_row = lax.broadcasted_iota(jnp.int32, (total,), 0) // block
    global_ids = slot_of_row * n_row + row_index
    solved_list = []
    for k in range(2):
        head = current.astype(jnp.float32)
        fan = lax.psum(head.astype(jnp.bfloat16), "col")
        local = jnp.dot(inverse_blocks[k], fan, preferred_element_type=jnp.float32).astype(
            jnp.bfloat16
        )
        arrived = spread(local, "row", k)
        solved_list.append(arrived)
        term = jnp.dot(panel[:, k, :], arrived, preferred_element_type=jnp.float32)
        newer = (current.astype(jnp.float32) - panel_scale[:, k : k + 1] * term).astype(
            jnp.bfloat16
        )
        current = jnp.where((global_ids > k)[:, None], newer, current)
    return (current[:, None, :], jnp.stack(solved_list))


def solution(mesh):
    placed = (P("row", "col", None), P("row", None, "col"), P("row", None), P(None, "col", None))
    return jax.shard_map(
        body,
        mesh=mesh,
        in_specs=placed,
        out_specs=(P("row", "col", None), P(None, "col", None)),
        check_vma=False,
    )
```

profile of v0, /device:TPU:8, one launch (start us, length us, event | category | flops | bytes accessed | tf_op | source)
XLA Modules:
  0.0 722.6 jit_solution(12241897476524964744)
XLA Ops:
  7.2 0.0 all-reduce.5.cloned.1.call-start
  7.2 3.9 copy.9
  11.2 0.0 copy-start.5
  11.2 0.0 copy-start.2
  11.2 0.0 all-reduce.5.cloned.1.call-update
  11.2 0.0 all-reduce.7.cloned.1.call-start
  11.3 0.6 copy-done.7
  11.9 0.0 copy-start
  11.9 82.6 %all-reduce.5.cloned.1.call-done = bf16[1024,1024]{0,1:T(8,128)(2,1)} async-done(((bf16[1024,1024]{0,1:T(8,128)(2,1)}), bf16[1024,1024]{0,1:T(8,128)(2,1)}) %all-reduce.5.cloned.1.call-update) | async-done | bytes 2097168 | tf_op jit(solution)/shard_map/psum | solution.py:23
  94.5 0.0 copy-done.5
  94.5 3.1 fusion.5
  97.6 0.0 all-reduce.7.cloned.1.call-update
  97.6 0.0 all-reduce.9.cloned.1.call-start
  97.7 0.0 copy-done.2
  97.7 1.5 fusion.19
  99.2 263.4 %all-reduce.7.cloned.1.call-done = bf16[128,1024]{1,0:T(8,128)(2,1)} async-done(((bf16[128,1024]{1,0:T(8,128)(2,1)}), bf16[128,1024]{1,0:T(8,128)(2,1)}) %all-reduce.7.cloned.1.call-update) | async-done | bytes 262160 | tf_op jit(solution)/shard_map/psum | solution.py:9
  362.6 0.0 copy-done
  362.6 3.3 fusion.2
  365.9 0.0 all-reduce.9.cloned.1.call-update
  365.9 0.0 copy-start.1
  365.9 0.0 all-reduce.11.cloned.1.call-start
  366.0 73.2 %all-reduce.9.cloned.1.call-done = bf16[1024,1024]{0,1:T(8,128)(2,1)} async-done(((bf16[1024,1024]{0,1:T(8,128)(2,1)}), bf16[1024,1024]{0,1:T(8,128)(2,1)}) %all-reduce.9.cloned.1.call-update) | async-done | bytes 2097168 | tf_op jit(solution)/shard_map/psum | solution.py:23
  439.2 0.0 copy-done.6
  439.2 3.1 fusion.7
  442.3 0.0 all-reduce.11.cloned.1.call-update
  442.4 265.7 %all-reduce.11.cloned.1.call-done = bf16[128,1024]{1,0:T(8,128)(2,1)} async-done(((bf16[128,1024]{1,0:T(8,128)(2,1)}), bf16[128,1024]{1,0:T(8,128)(2,1)}) %all-reduce.11.cloned.1.call-update) | async-done | bytes 262160 | tf_op jit(solution)/shard_map/psum | solution.py:9
  708.1 0.0 copy-done.1
  708.1 3.1 fusion.4
  711.3 4.0 copy.13
  715.3 0.0 copy-done.3
  715.3 0.0 copy-done.4
  715.3 0.8 pad_maximum_fusion
  (7 shorter events, 0.0 us)
Async XLA Ops:
  7.2 87.3 %all-reduce.5.cloned.1.call-start = ((), (), s32[]{:S(2)}) async-start(), calls=%async_computation | async-start | bytes 4194304 | tf_op jit(solution)/shard_map/psum | solution.py:23
  11.2 0.7 copy-start.7
  11.2 83.3 %copy-start.5 = (bf16[2,128,1024]{2,1,0:T(8,128)(2,1)S(1)}, bf16[2,128,1024]{2,1,0:T(8,128)(2,1)}, u32[]{:S(2)}) copy-start(bf16[2,128,1024]{2,1,0:T(8,128)(2,1)} %param.7) | copy-start | bytes 1572868
  11.2 86.5 %copy-start.2 = (bf16[1024,2,128]{2,1,0:T(2,128)(2,1)S(1)}, bf16[1024,2,128]{2,1,0:T(2,128)(2,1)}, u32[]{:S(2)}) copy-start(bf16[1024,2,128]{2,1,0:T(2,128)(2,1)} %param.5) | copy-start | bytes 1572868
  11.2 351.4 %all-reduce.7.cloned.1.call-start = ((), (), s32[]{:S(2)}) async-start(), calls=%async_computation.1 | async-start | bytes 524288 | tf_op jit(solution)/shard_map/psum | solution.py:9
  11.9 350.7 %copy-start = (bf16[1024,1,1024]{0,2,1:T(8,128)(2,1)S(1)}, bf16[1024,1,1024]{0,2,1:T(8,128)(2,1)}, u32[]{:S(2)}) copy-start(bf16[1024,1,1024]{0,2,1:T(8,128)(2,1)} %copy.9) | copy-start | bytes 6291460
  97.6 341.6 %all-reduce.9.cloned.1.call-start = ((), (), s32[]{:S(2)}) async-start(), calls=%async_computation.2 | async-start | bytes 4194304 | tf_op jit(solution)/shard_map/psum | solution.py:23
  365.9 73.3 %copy-start.6 = (bf16[2,128,1024]{2,1,0:T(8,128)(2,1)S(1)}, bf16[2,128,1024]{2,1,0:T(8,128)(2,1)}, u32[]{:S(2)}) copy-start(bf16[2,128,1024]{2,1,0:T(8,128)(2,1)} %param.7) | copy-start | bytes 1572868
  365.9 342.2 %copy-start.1 = (bf16[1024,1024]{0,1:T(8,128)(2,1)S(1)}, bf16[1024,1024]{0,1:T(8,128)(2,1)}, u32[]{:S(2)}) copy-start(bf16[1024,1024]{0,1:T(8,128)(2,1)} %fusion.2) | copy-start | bytes 6291460
  365.9 342.2 %all-reduce.11.cloned.1.call-start = ((), (), s32[]{:S(2)}) async-start(), calls=%async_computation.3 | async-start | bytes 524288 | tf_op jit(solution)/shard_map/psum | solution.py:9
  711.3 4.0 copy-start.3
  711.3 4.0 copy-start.4
Sparse Core Ops, SparseCore 0:
  11.3 83.1 all-reduce.4
  97.9 264.6 all-reduce.6
  366.0 73.1 all-reduce.8
  443.5 264.6 all-reduce.10
where the time goes:
time: 723 us
  waiting for transfers between devices  685 us (95%)
  between operations  13.8 us (2%)
  matrix products  12.7 us (2%)
  local copies, waits for them, and re-layouts  10.1 us (1%)
    psum x2, waiting for transfers between devices, spread(): return lax.psum(jnp.where(mine, shard, jnp.zeros_like(shard)), axis)  529 us
    psum x2, waiting for transfers between devices, body(): fan = lax.psum(head.astype(jnp.bfloat16), 'col')  156 us
  transfers between devices with their start and end apart: 4, of which 4 were waited for; matrix products, arithmetic and copies ran while one was open for 0% of the time, Pallas kernels for 0%

commit v1 on v0

--- a/solution.py
+++ b/solution.py
@@ -4,9 +4,15 @@
 from jax.sharding import PartitionSpec as P
 
 
+def summed_here(x, name):
+    parts = lax.all_gather(x, name, axis=0, tiled=False)
+    summed = parts.sum(axis=0)
+    return summed
+
+
 def spread(shard, axis, root):
     mine = lax.axis_index(axis) == root
-    return lax.psum(jnp.where(mine, shard, jnp.zeros_like(shard)), axis)
+    return summed_here(jnp.where(mine, shard, jnp.zeros_like(shard)), axis)
 
 
 def body(pending, panel, panel_scale, inverse_blocks):

time: 723 us -> 636 us (0.88)
  the two profiles are of different devices: /device:TPU:8 before, /device:TPU:2 now
where the time goes in v1:
time: 636 us; the launch traced here: 635 us
  waiting for transfers between devices  574 us (90%)
  other arithmetic  18.5 us (3%)
  local copies, waits for them, and re-layouts  18.4 us (3%)
  between operations  13.9 us (2%)
  matrix products  10.5 us (2%)
    all_gather x2, waiting for transfers between devices, summed_here(): parts = lax.all_gather(x, name, axis=0, tiled=False)  409 us
    psum x2, waiting for transfers between devices, body(): fan = lax.psum(head.astype(jnp.bfloat16), 'col')  165 us
    reduce_sum x2, other arithmetic, summed_here(): summed = parts.sum(axis=0)  17.6 us
    unnamed x15, local copies, waits for them, and re-layouts  17.6 us
  transfers between devices with their start and end apart: 4, of which 4 were waited for; matrix products, arithmetic and copies ran while one was open for 0% of the time, Pallas kernels for 0%

profile of v1, /device:TPU:2, one launch (start us, length us, event | category | flops | bytes accessed | tf_op | source)
XLA Modules:
  0.0 635.3 jit_solution(14211045408822969333)
XLA Ops:
  7.2 0.0 all-reduce.3.cloned.1.call-start
  7.2 3.9 copy.17
  11.2 0.0 copy-start.3
  11.2 0.0 all-reduce.3.cloned.1.call-update
  11.2 0.0 all-gather.5.cloned.1.call-start
  11.2 85.7 %all-reduce.3.cloned.1.call-done = bf16[1024,1024]{0,1:T(8,128)(2,1)} async-done(((bf16[1024,1024]{0,1:T(8,128)(2,1)}), bf16[1024,1024]{0,1:T(8,128)(2,1)}) %all-reduce.3.cloned.1.call-update) | async-done | bytes 2097168 | tf_op jit(solution)/shard_map/psum | solution.py:29
  96.9 0.0 copy-done.3
  96.9 3.1 fusion.5
  100.1 0.0 all-gather.5.cloned.1.call-update
  100.1 0.0 all-reduce.5.cloned.1.call-start
  100.2 0.0 copy-done.5
  100.2 0.0 copy-done.2
  100.2 0.7 fusion.19
  100.9 191.6 %all-gather.5.cloned.1.call-done = bf16[8192,1024]{1,0:T(8,128)(2,1)} async-done(((bf16[128,1024]{1,0:T(8,128)(2,1)}), bf16[8192,1024]{1,0:T(8,128)(2,1)}) %all-gather.5.cloned.1.call-update) | async-done | bytes 16777232 | tf_op jit(solution)/shard_map/all_gather | solution.py:8
  292.5 9.1 %reduce_sum.24 = bf16[128,1024]{1,0:T(8,128)(2,1)S(1)} reduce(bf16[64,128,1024]{2,1,0:T(8,128)(2,1)} %bitcast.46, bf16[]{:T(256)} %constant.36.clone.1), dimensions={0}, to_apply=%region_1.2 | reduce | flops 8257536 | bytes 17039362 | tf_op jit(solution)/shard_map/reduce_sum | solution.py:9
  301.6 0.0 copy-done
  301.6 2.2 fusion.2
  303.8 0.0 all-reduce.5.cloned.1.call-update
  303.8 0.0 all-gather.7.cloned.1.call-start
  303.9 78.9 %all-reduce.5.cloned.1.call-done = bf16[1024,1024]{0,1:T(8,128)(2,1)} async-done(((bf16[1024,1024]{0,1:T(8,128)(2,1)}), bf16[1024,1024]{0,1:T(8,128)(2,1)}) %all-reduce.5.cloned.1.call-update) | async-done | bytes 2097168 | tf_op jit(solution)/shard_map/psum | solution.py:29
  382.8 0.0 copy-done.4
  382.8 3.0 fusion.7
  385.8 0.0 all-gather.7.cloned.1.call-update
  385.8 217.6 %all-gather.7.cloned.1.call-done = bf16[8192,1024]{0,1:T(8,128)(2,1)} async-done(((bf16[128,1024]{0,1:T(8,128)(2,1)}), bf16[8192,1024]{0,1:T(8,128)(2,1)}) %all-gather.7.cloned.1.call-update) | async-done | bytes 16777232 | tf_op jit(solution)/shard_map/all_gather | solution.py:8
  603.4 9.7 %copy.24 = bf16[128,8,64,128]{3,2,1,0:T(8,128)(2,1)S(1)} copy(bf16[128,8,64,128]{3,1,2,0:T(8,128)(2,1)} %bitcast.47) | data formatting | bytes 33554432
  613.1 0.0 copy-start.1
  613.1 8.5 %bitcast_reduce_fusion = bf16[128,1024]{0,1:T(8,128)(2,1)S(1)} fusion(bf16[128,8,64,128]{3,2,1,0:T(8,128)(2,1)S(1)} %copy.24), kind=kLoop, calls=%fused_computation | loop fusion | flops 8257536 | bytes 17039360 | tf_op jit(solution)/shard_map/reduce_sum | solution.py:9
  621.6 0.1 copy.20
  621.8 0.0 copy-done.1
  621.8 2.2 fusion.4
  623.9 3.9 copy.21
  627.9 0.8 pad_maximum_fusion
  (7 shorter events, 0.0 us)
Async XLA Ops:
  7.2 89.8 %all-reduce.3.cloned.1.call-start = ((), (), s32[]{:S(2)}) async-start(), calls=%async_computation | async-start | bytes 4194304 | tf_op jit(solution)/shard_map/psum | solution.py:29
  11.2 85.8 %copy-start.3 = (bf16[2,128,1024]{2,1,0:T(8,128)(2,1)S(1)}, bf16[2,128,1024]{2,1,0:T(8,128)(2,1)}, u32[]{:S(2)}) copy-start(bf16[2,128,1024]{2,1,0:T(8,128)(2,1)} %param.7) | copy-start | bytes 1572868
  11.2 89.0 %copy-start.5 = (f32[1024,2]{0,1:T(2,128)S(1)}, f32[1024,2]{0,1:T(2,128)}, u32[]{:S(2)}) copy-start(f32[1024,2]{0,1:T(2,128)} %param.6) | copy-start | bytes 24580
  11.2 89.0 %copy-start.2 = (bf16[1024,2,128]{2,1,0:T(2,128)(2,1)S(1)}, bf16[1024,2,128]{2,1,0:T(2,128)(2,1)}, u32[]{:S(2)}) copy-start(bf16[1024,2,128]{2,1,0:T(2,128)(2,1)} %param.5) | copy-start | bytes 1572868
  11.2 281.3 %all-gather.5.cloned.1.call-start = ((), (), s32[]{:S(2)}) async-start(), calls=%async_computation.2 | async-start | bytes 17039360 | tf_op jit(solution)/shard_map/all_gather | solution.py:8
  100.1 282.7 %all-reduce.5.cloned.1.call-start = ((), (), s32[]{:S(2)}) async-start(), calls=%async_computation.1 | async-start | bytes 4194304 | tf_op jit(solution)/shard_map/psum | solution.py:29
  292.5 9.1 %copy-start = (bf16[1024,1,1024]{0,2,1:T(8,128)(2,1)S(1)}, bf16[1024,1,1024]{0,2,1:T(8,128)(2,1)}, u32[]{:S(2)}) copy-start(bf16[1024,1,1024]{0,2,1:T(8,128)(2,1)} %copy.17) | copy-start | bytes 6291460
  303.8 79.0 %copy-start.4 = (bf16[2,128,1024]{2,1,0:T(8,128)(2,1)S(1)}, bf16[2,128,1024]{2,1,0:T(8,128)(2,1)}, u32[]{:S(2)}) copy-start(bf16[2,128,1024]{2,1,0:T(8,128)(2,1)} %param.7) | copy-start | bytes 1572868
  303.8 299.6 %all-gather.7.cloned.1.call-start = ((), (), s32[]{:S(2)}) async-start(), calls=%async_computation.3 | async-start | bytes 17039360 | tf_op jit(solution)/shard_map/all_gather | solution.py:8
  613.1 8.7 %copy-start.1 = (bf16[1024,1024]{0,1:T(8,128)(2,1)S(1)}, bf16[1024,1024]{0,1:T(8,128)(2,1)}, u32[]{:S(2)}) copy-start(bf16[1024,1024]{0,1:T(8,128)(2,1)} %fusion.2) | copy-start | bytes 6291460
Sparse Core Ops, SparseCore 0:
  11.3 85.5 all-reduce.2
  100.5 191.9 all-gather.4
  304.0 78.7 all-reduce.4
  386.1 217.2 all-gather.6
